TPU v7x, 512 devices: a whole 4x8x8 slice. The times are simulated.
512 devices in a mesh: seq: 64 (over y, z), head: 8 (over x, core).
Axes of the slice: x: 4, y: 8, z: 8, core: 2. Of those that a mesh axis runs over, the one named last changes fastest.
Arguments:
- queries: bfloat16 [16384, 4096], P(('seq', 'head'))
- key_values: bfloat16 [16384, 2, 1024], P(('seq', 'head'))
- gate_logits: bfloat16 [16384, 4096], P(('seq', 'head')), may hold values from -6 to 6
- vertical_blocks: int32 [32, 16], replicated, may hold values from 0 to 255, as said below
- slash_offsets: int32 [32, 8], replicated, may hold values from 0 to 8, as said below
- slash_count: int32 [32], replicated, may hold values from 2 to 8, as said below
Outputs:
- gated: bfloat16 [16384, 4096], P(('seq', 'head'))
Inputs may be any that keep to these rules, and one draw needn't show every extreme that they name: `slash_count`: between 2 and 8; the largest and the smallest are reached. Heads are ranked by (slash_count[h], h) ascending, and rank r goes to head group (r % 8) if (r // 8) is even, else to group 8 - 1 - (r % 8). For each head, slash_offsets[h, 0] = 0 and the 8 offsets are distinct; the largest possible offset is used by some head. `vertical_blocks`: each head's 16 blocks lie in distinct token shards of 256 tokens (block b is in shard b // 4); the heads of one group, as defined with slash_count, have at most 1 vertical blocks in one shard together, and exactly 1 in some shard. The first and the last block of the stretch are used by some head.
All inputs are finite; a program needn't handle non-finite values.
Results may differ from a plain program's by a relative error of at most 0.0057.
Values may be sent and summed in bfloat16 or wider, within the bound.
No kernel may reach another device: no remote copies, remote signals or barrier semaphores. Data moves between devices by JAX's collectives and lax.ppermute only.
A program may use at most 64 MiB of HBM per device.

v0:
```python
import jax
import jax.numpy as jnp
from jax import lax
from jax.sharding import PartitionSpec as P

H = 32
KVH = 8
DH = 128
BLOCK = 64
NS = 8
REACH = 2


def from_behind(value, axis, steps):
    count = lax.axis_size(axis)
    first, last = (max(0, -steps), min(count, count - steps))
    return lax.ppermute(value, axis, [(source, source + steps) for source in range(first, last)])


def block_attend(
    q_rows,
    vert_keys,
    vert_vals,
    vert_ids,
    vert_live,
    slash_keys,
    slash_vals,
    offsets,
    slash_live,
    block_index,
):
    head_width = q_rows.shape[-1]
    score_scale = head_width ** (-0.5)
    positions = jnp.arange(q_rows.shape[0], dtype=jnp.int32)
    causal = positions[None, :] <= positions[:, None]
    vert_scores = (
        jnp.einsum("qd,skd->qsk", q_rows, vert_keys, preferred_element_type=jnp.float32)
        * score_scale
    )
    slash_scores = (
        jnp.einsum("qd,nkd->qnk", q_rows, slash_keys, preferred_element_type=jnp.float32)
        * score_scale
    )
    distance = block_index - vert_ids
    on_slash = jnp.any((distance[:, None] == offsets[None, :]) & slash_live[None, :], axis=1)
    vert_ok = vert_live & (vert_ids >= 0) & (vert_ids <= block_index) & jnp.logical_not(on_slash)
    vert_mask = vert_ok[None, :, None] & (
        (vert_ids < block_index)[None, :, None] | causal[:, None, :]
    )
    slash_ok = slash_live & (block_index - offsets >= 0)
    slash_mask = slash_ok[None, :, None] & ((offsets > 0)[None, :, None] | causal[:, None, :])
    vert_scores = jnp.where(vert_mask, vert_scores, -jnp.inf)
    slash_scores = jnp.where(slash_mask, slash_scores, -jnp.inf)
    row_max = jnp.maximum(jnp.max(vert_scores, axis=(1, 2)), jnp.max(slash_scores, axis=(1, 2)))
    vert_exp = jnp.exp(vert_scores - row_max[:, None, None])
    slash_exp = jnp.exp(slash_scores - row_max[:, None, None])
    row_total = jnp.sum(vert_exp, axis=(1, 2)) + jnp.sum(slash_exp, axis=(1, 2))
    vert_weight = (vert_exp / row_total[:, None, None]).astype(jnp.bfloat16)
    slash_weight = (slash_exp / row_total[:, None, None]).astype(jnp.bfloat16)
    result = jnp.einsum("qsk,skd->qd", vert_weight, vert_vals, preferred_element_type=jnp.float32)
    result = result + jnp.einsum(
        "qnk,nkd->qd", slash_weight, slash_vals, preferred_element_type=jnp.float32
    )
    return result.astype(jnp.bfloat16)


def group_order(counts, group_count):
    group_size = H // group_count
    ranking = jnp.argsort(counts * H + jnp.arange(H, dtype=jnp.int32), stable=True)
    index = jnp.arange(H, dtype=jnp.int32)
    group = index // group_size
    within = index % group_size
    rank_of = within * group_count + jnp.where(within % 2 == 0, group, group_count - 1 - group)
    return ranking[rank_of]


def body(queries, key_values, gate_logits, vertical_blocks, slash_offsets, slash_count):
    group_count = lax.axis_size("head")
    seq_rank = lax.axis_index("seq")
    group_rank = lax.axis_index("head")
    group_size = H // group_count
    tok_rows = queries.shape[0]
    tok_dev = tok_rows * group_count
    blocks_dev = tok_dev // BLOCK
    head_slot = group_order(slash_count, group_count)
    kv_index = head_slot // (H // KVH)
    my_heads = lax.dynamic_slice_in_dim(head_slot, group_rank * group_size, group_size)
    q_grouped = jnp.take(queries.reshape(tok_rows, H, DH), head_slot, axis=1)
    my_queries = lax.all_to_all(q_grouped, "head", split_axis=1, concat_axis=0, tiled=True)
    whole_pairs = lax.all_gather(key_values, "head", axis=0, tiled=True)
    my_kv = lax.dynamic_slice_in_dim(kv_index, group_rank * group_size, group_size)
    my_pairs = jnp.take(whole_pairs.reshape(tok_dev, 2, KVH, DH), my_kv, axis=2)
    earlier = []
    for distance in range(REACH, 0, -1):
        earlier.append(from_behind(my_pairs, "seq", distance))
    reach_keys = jnp.concatenate(earlier + [my_pairs], axis=0)
    reach_blocks = reach_keys.reshape((REACH + 1) * blocks_dev, BLOCK, 2, group_size, DH)
    pair_blocks = my_pairs.reshape(blocks_dev, BLOCK, 2, group_size, DH)
    my_vertical = jnp.take(vertical_blocks, my_heads, axis=0)
    owned = my_vertical // blocks_dev == seq_rank
    block_range = jnp.arange(blocks_dev, dtype=jnp.int32)
    owned_ids = jnp.max(jnp.where(owned, my_vertical, -1), axis=1)
    local_block = owned_ids - seq_rank * blocks_dev
    selector = ((local_block[:, None] == block_range[None, :]) & (owned_ids >= 0)[:, None]).astype(
        jnp.bfloat16
    )
    packed = jnp.einsum(
        "pt,tbxpd->pxbd", selector, pair_blocks, preferred_element_type=jnp.float32
    ).astype(jnp.bfloat16)
    vert_data, vert_all_ids = (
        lax.all_gather(packed[None], "seq", axis=0, tiled=True),
        lax.all_gather(owned_ids[None], "seq", axis=0, tiled=True),
    )

    def vertical_for(head_pos):
        chosen = lax.dynamic_index_in_dim(vert_data, head_pos, 1, keepdims=False)
        chosen_ids = lax.dynamic_index_in_dim(vert_all_ids, head_pos, 1, keepdims=False)
        return (chosen[:, 0], chosen[:, 1], chosen_ids, jnp.ones(chosen_ids.shape, dtype=bool))

    slot_range_ns = jnp.arange(NS, dtype=jnp.int32)
    my_offsets = jnp.take(slash_offsets, my_heads, axis=0)
    my_counts = jnp.take(slash_count, my_heads, axis=0)

    def head_pass(head_pos):
        vert_keys, vert_vals, vert_ids, vert_live = vertical_for(head_pos)
        head_queries = lax.dynamic_index_in_dim(my_queries, head_pos, 1, keepdims=False).reshape(
            blocks_dev, BLOCK, DH
        )
        head_reach = lax.dynamic_index_in_dim(reach_blocks, head_pos, 3, keepdims=False)
        offsets = lax.dynamic_index_in_dim(my_offsets, head_pos, 0, keepdims=False)
        slash_live = slot_range_ns < lax.dynamic_index_in_dim(
            my_counts, head_pos, 0, keepdims=False
        )

        def query_pass(inputs):
            q_rows, local_index = inputs
            block_index = seq_rank * blocks_dev + local_index
            slash_index = REACH * blocks_dev + local_index - offsets
            slash_blocks = jnp.take(head_reach, slash_index, axis=0)
            return block_attend(
                q_rows,
                vert_keys,
                vert_vals,
                vert_ids,
                vert_live,
                slash_blocks[:, :, 0],
                slash_blocks[:, :, 1],
                offsets,
                slash_live,
                block_index,
            )

        return lax.map(query_pass, (head_queries, block_range))

    attended = lax.map(head_pass, jnp.arange(group_size, dtype=jnp.int32)).reshape(
        group_size, tok_dev, DH
    )
    returned = lax.all_to_all(attended, "head", split_axis=1, concat_axis=0, tiled=True)
    head_range_all = jnp.arange(H, dtype=jnp.int32)
    inverse = jnp.sum(
        jnp.where(head_slot[None, :] == head_range_all[:, None], head_range_all[None, :], 0), axis=1
    )
    natural = jnp.take(returned, inverse, axis=0)
    gate = jax.nn.sigmoid(gate_logits.astype(jnp.float32)).reshape(tok_rows, H, DH)
    gated = gate * jnp.transpose(natural, (1, 0, 2)).astype(jnp.float32)
    return gated.astype(jnp.bfloat16).reshape(tok_rows, H * DH)


def solution(mesh):
    in_specs = (
        P(("seq", "head"), None),
        P(("seq", "head"), None, None),
        P(("seq", "head"), None),
        P(),
        P(),
        P(),
    )
    out_specs = P(("seq", "head"), None)
    return jax.shard_map(body, mesh=mesh, in_specs=in_specs, out_specs=out_specs, check_vma=False)
```

profile of v0, /device:TPU:1, one launch (start us, length us, event | category | flops | bytes accessed | tf_op | source)
XLA Modules:
  0.0 331.5 jit_solution(11809386844297845460)
XLA Ops:
  8.7 1.6 sort.17
  12.1 32.1 %all-gather.5.cloned.1.call-done = bf16[256,2,1024]{2,1,0:T(2,128)(2,1)} async-done(((bf16[32,2,1024]{2,1,0:T(2,128)(2,1)}), bf16[256,2,1024]{2,1,0:T(2,128)(2,1)}) %all-gather.5.cloned.1.call-update) | async-done | bytes 1048592 | tf_op jit(solution)/shard_map/all_gather | solution.py:90
  44.1 2.4 copy.60
  49.9 0.8 select_bitcast_fusion
  50.7 3.6 %all-to-all-start = ((bf16[32,32,128]{2,0,1:T(8,128)(2,1)}), bf16[32,32,128]{2,0,1:T(8,128)(2,1)S(1)}, u32[]{:S(2)}, u32[]{:S(2)}) async-start(bf16[32,32,128]{2,0,1:T(8,128)(2,1)} %select_bitcast_fusion), calls=%async_computation | async-start | bytes 524288 | tf_op jit(solution)/shard_map/all_to_all | solution.py:89
  55.1 4.2 %collective-permute-start = (bf16[256,2,4,128]{3,0,1,2:T(8,128)(2,1)S(1)}, bf16[256,2,4,128]{3,0,1,2:T(8,128)(2,1)S(1)}, u32[]{:S(2)}, u32[]{:S(2)}) collective-permute-start(bf16[256,2,4,128]{3,0,1,2:T(8,128)(2,1)S(1)} %bitcast_select_fusion), channel_id=1, source_target_pairs={{0,16},{8,24},{16,32},{24,40},{32,48},{40,56},{48,64},{56,72},{64,... | collective-permute-start | bytes 1572872 | tf_op jit(solution)/shard_map/ppermute | solution.py:17
  59.3 3.3 collective-permute-start.1
  62.8 1.3 dynamic-slice
  64.9 45.2 %all-reduce = s32[256]{0:T(256)S(1)} all-reduce(s32[256]{0:T(256)S(1)} %dynamic-update-slice), channel_id=3, replica_groups=mesh['seq'=64,'head'=8] {'seq'}, use_global_device_ids=true, to_apply=%add | all-reduce | flops 256 | bytes 2048
  111.0 1.3 pad_maximum_fusion
  112.4 60.5 %all-gather.7.cloned.1.call-done = bf16[256,2,64,128]{3,2,1,0:T(8,128)(2,1)} async-done(((bf16[4,2,64,128]{3,2,1,0:T(8,128)(2,1)}), bf16[256,2,64,128]{3,2,1,0:T(8,128)(2,1)}) %all-gather.7.cloned.1.call-update) | async-done | bytes 8388624 | tf_op jit(solution)/shard_map/all_gather | solution.py:111
  172.9 136.7 %while.37 = (s32[]{:T(128)}, bf16[4,4,64,128]{3,2,1,0:T(8,128)(2,1)}, s32[4]{0:T(128)S(1)}, bf16[256,4,128]{2,0,1:T(8,128)(2,1)S(1)}, s32[4,8]{1,0:T(4,128)S(1)}...) while((s32[]{:T(128)}, ...), condition=%wide.region_11.12_spmd.clone.clone, body=%wide.region_3.11_spmd.clone.clone.sunk | while | flops 154098576 | bytes 21907556 | solution.py:155
  175.1 1.8 copy_bitcast_fusion.6
  176.9 1.5 slice_bitcast_fusion.8
  178.4 1.0 copy_bitcast_fusion.7
  180.7 25.7 %while.38 = (s32[]{:T(128)}, bf16[4,64,128]{2,1,0:T(8,128)(2,1)S(1)}, s32[64]{0:T(128)S(1)}, s32[4]{0:T(128)S(1)}, s32[]{:T(128)}, /*index=5*/s32[8]{0:T(128)S(1...) while((s32[]{:T(128)}, ...), condition=%wide.region_10.10_spmd, body=%wide.region_4.9_spmd.sunk | while | flops 154098560 | bytes 12468941 | solution.py:153
  182.1 1.9 fusion.56
  188.5 1.9 fusion.56
  194.9 1.9 fusion.56
  201.4 1.9 fusion.56
  209.3 1.8 copy_bitcast_fusion.6
  211.1 1.5 slice_bitcast_fusion.8
  212.5 1.0 copy_bitcast_fusion.7
  214.9 25.7 %while.38 = (s32[]{:T(128)}, bf16[4,64,128]{2,1,0:T(8,128)(2,1)S(1)}, s32[64]{0:T(128)S(1)}, s32[4]{0:T(128)S(1)}, s32[]{:T(128)}, /*index=5*/s32[8]{0:T(128)S(1...) while((s32[]{:T(128)}, ...), condition=%wide.region_10.10_spmd, body=%wide.region_4.9_spmd.sunk | while | flops 154098560 | bytes 12468941 | solution.py:153
  216.2 1.9 fusion.56
  222.7 1.9 fusion.56
  229.1 1.9 fusion.56
  235.5 1.9 fusion.56
  243.5 1.8 copy_bitcast_fusion.6
  245.2 1.5 slice_bitcast_fusion.8
  246.7 1.0 copy_bitcast_fusion.7
  249.0 25.7 %while.38 = (s32[]{:T(128)}, bf16[4,64,128]{2,1,0:T(8,128)(2,1)S(1)}, s32[64]{0:T(128)S(1)}, s32[4]{0:T(128)S(1)}, s32[]{:T(128)}, /*index=5*/s32[8]{0:T(128)S(1...) while((s32[]{:T(128)}, ...), condition=%wide.region_10.10_spmd, body=%wide.region_4.9_spmd.sunk | while | flops 154098560 | bytes 12468941 | solution.py:153
  250.4 1.9 fusion.56
  256.8 1.9 fusion.56
  263.3 1.9 fusion.56
  269.7 1.9 fusion.56
  277.6 1.8 copy_bitcast_fusion.6
  279.4 1.5 slice_bitcast_fusion.8
  280.9 1.0 copy_bitcast_fusion.7
  283.2 25.7 %while.38 = (s32[]{:T(128)}, bf16[4,64,128]{2,1,0:T(8,128)(2,1)S(1)}, s32[64]{0:T(128)S(1)}, s32[4]{0:T(128)S(1)}, s32[]{:T(128)}, /*index=5*/s32[8]{0:T(128)S(1...) while((s32[]{:T(128)}, ...), condition=%wide.region_10.10_spmd, body=%wide.region_4.9_spmd.sunk | while | flops 154098560 | bytes 12468941 | solution.py:153
  284.6 1.9 fusion.56
  291.0 1.9 fusion.56
  297.5 1.9 fusion.56
  303.9 1.9 fusion.56
  309.6 1.9 copy.66
  311.5 5.2 %all-to-all-start.1 = ((bf16[4,256,128]{2,0,1:T(4,128)(2,1)}), bf16[4,256,128]{2,0,1:T(4,128)(2,1)S(1)}, u32[]{:S(2)}, u32[]{:S(2)}) async-start(bf16[4,256,128]{2,0,1:T(4,128)(2,1)} %bitcast.26), calls=%async_computation.1 | async-start | bytes 524288 | tf_op jit(solution)/shard_map/all_to_all | solution.py:158
  316.7 6.4 %all-to-all-done.1 = bf16[4,256,128]{2,0,1:T(4,128)(2,1)S(1)} async-done(((bf16[4,256,128]{2,0,1:T(4,128)(2,1)}), bf16[4,256,128]{2,0,1:T(4,128)(2,1)S(1)}, u32[]{:S(2)}, u32[]{:S(2)}) %all-to-all-start.1) | async-done | bytes 262176 | tf_op jit(solution)/shard_map/all_to_all | solution.py:158
  323.8 0.9 copy_bitcast_fusion.2
  (396 shorter events, 70.7 us)
Async XLA Ops:
  6.5 42.7 %copy-start = (bf16[32,4096]{1,0:T(8,128)(2,1)S(1)}, bf16[32,4096]{1,0:T(8,128)(2,1)}, u32[]{:S(2)}) copy-start(bf16[32,4096]{1,0:T(8,128)(2,1)} %param.10) | copy-start | bytes 786436
  6.5 37.6 %all-gather.5.cloned.1.call-start = ((), (), s32[]{:S(2)}) async-start(), calls=%async_computation.2 | async-start | bytes 1179648 | tf_op jit(solution)/shard_map/all_gather | solution.py:90
  7.3 165.6 %all-gather.7.cloned.1.call-start = ((), (), s32[]{:S(2)}) async-start(), calls=%async_computation.3 | async-start | bytes 8519680 | tf_op jit(solution)/shard_map/all_gather | solution.py:111
  48.0 6.3 %copy-start.1 = (s32[32]{0:T(128)S(1)}, s32[32]{0:T(128)}, u32[]{:S(2)}) copy-start(s32[32]{0:T(128)} %param.15) | copy-start | bytes 388
  48.5 61.8 %copy-start.4 = (s32[32,8]{0,1:T(8,128)S(1)}, s32[32,8]{0,1:T(8,128)}, u32[]{:S(2)}) copy-start(s32[32,8]{0,1:T(8,128)} %param.14) | copy-start | bytes 3076
  50.7 60.3 %all-to-all-start = ((bf16[32,32,128]{2,0,1:T(8,128)(2,1)}), bf16[32,32,128]{2,0,1:T(8,128)(2,1)S(1)}, u32[]{:S(2)}, u32[]{:S(2)}) async-start(bf16[32,32,128]{2,0,1:T(8,128)(2,1)} %select_bitcast_fusion), calls=%async_computation | async-start | bytes 524288 | tf_op jit(solution)/shard_map/all_to_all | solution.py:89
  55.1 55.9 %collective-permute-start = (bf16[256,2,4,128]{3,0,1,2:T(8,128)(2,1)S(1)}, bf16[256,2,4,128]{3,0,1,2:T(8,128)(2,1)S(1)}, u32[]{:S(2)}, u32[]{:S(2)}) collective-permute-start(bf16[256,2,4,128]{3,0,1,2:T(8,128)(2,1)S(1)} %bitcast_select_fusion), channel_id=1, source_target_pairs={{0,16},{8,24},{16,32},{24,40},{32,48},{40,56},{48,64},{56,72},{64,... | collective-permute-start | bytes 1572872 | tf_op jit(solution)/shard_map/ppermute | solution.py:17
  59.3 51.7 %collective-permute-start.1 = (bf16[256,2,4,128]{3,0,1,2:T(8,128)(2,1)S(1)}, bf16[256,2,4,128]{3,0,1,2:T(8,128)(2,1)S(1)}, u32[]{:S(2)}, u32[]{:S(2)}) collective-permute-start(bf16[256,2,4,128]{3,0,1,2:T(8,128)(2,1)S(1)} %bitcast_select_fusion), channel_id=1, source_target_pairs={{0,8},{8,16},{16,24},{24,32},{32,40},{40,48},{48,56},{56,64},{64,7... | collective-permute-start | bytes 1572872 | tf_op jit(solution)/shard_map/ppermute | solution.py:17
  185.4 1.2 copy-start.2
  191.8 1.2 copy-start.2
  198.2 1.2 copy-start.2
  204.7 1.2 copy-start.2
  219.5 1.2 copy-start.2
  226.0 1.2 copy-start.2
  232.4 1.2 copy-start.2
  238.8 1.2 copy-start.2
  253.7 1.2 copy-start.2
  260.1 1.2 copy-start.2
  266.6 1.2 copy-start.2
  273.0 1.2 copy-start.2
  287.9 1.2 copy-start.2
  294.3 1.2 copy-start.2
  300.8 1.2 copy-start.2
  307.2 1.2 copy-start.2
  309.6 14.2 %copy-start.3 = (bf16[32,4096]{1,0:T(8,128)(2,1)S(1)}, bf16[32,4096]{1,0:T(8,128)(2,1)}, u32[]{:S(2)}) copy-start(bf16[32,4096]{1,0:T(8,128)(2,1)} %param.12) | copy-start | bytes 786436
  311.5 11.6 %all-to-all-start.1 = ((bf16[4,256,128]{2,0,1:T(4,128)(2,1)}), bf16[4,256,128]{2,0,1:T(4,128)(2,1)S(1)}, u32[]{:S(2)}, u32[]{:S(2)}) async-start(bf16[4,256,128]{2,0,1:T(4,128)(2,1)} %bitcast.26), calls=%async_computation.1 | async-start | bytes 524288 | tf_op jit(solution)/shard_map/all_to_all | solution.py:158
Sparse Core Ops, SparseCore 0:
  9.5 34.5 all-gather.4
  49.3 123.5 all-gather.6
where the time goes:
time: 334 us; the launch traced here: 332 us
  waiting for transfers between devices  99.8 us (30%)
  local copies, waits for them, and re-layouts  57.9 us (17%)
  matrix products  47.2 us (14%)
  blocking collectives  45.2 us (14%)
  loops' own time  27.9 us (8%)
  other arithmetic  23.1 us (7%)
  starting transfers between devices  16.3 us (5%)
  between operations  14.3 us (4%)
    all_gather x1, waiting for transfers between devices, body(): lax.all_gather(packed[None], 'seq', axis=0, tiled=True)  60.5 us
    unnamed x1, blocking collectives  45.2 us
    all_gather x1, waiting for transfers between devices, body(): whole_pairs = lax.all_gather(key_values, 'head', axis=0, tiled=True)  32.1 us
    dot_general x16, matrix products, block_attend(): jnp.einsum('qd,skd->qsk', q_rows, vert_keys, preferred_element_type=jnp.f...  30.9 us
    another operation x4, loops' own time, head_pass(): return lax.map(query_pass, (head_queries, block_range))  21 us
    dynamic_slice x20, local copies, waits for them, and re-layouts, body(): lax.map(head_pass, jnp.arange(group_size, dtype=jnp.int32))  12.1 us
    reduce_sum x32, other arithmetic, block_attend(): row_total = jnp.sum(vert_exp, axis=(1, 2)) + jnp.sum(slash_exp, axis=(1, 2))  10.5 us
    gather x16, local copies, waits for them, and re-layouts, query_pass(): slash_blocks = jnp.take(head_reach, slash_index, axis=0)  9.56 us
  transfers between devices with their start and end apart: 6, of which 3 were waited for; matrix products, arithmetic and copies ran while one was open for 3% of the time, Pallas kernels for 0%

commit v1 on v0

--- a/solution.py
+++ b/solution.py
@@ -87,7 +87,9 @@
     my_heads = lax.dynamic_slice_in_dim(head_slot, group_rank * group_size, group_size)
     q_grouped = jnp.take(queries.reshape(tok_rows, H, DH), head_slot, axis=1)
     my_queries = lax.all_to_all(q_grouped, "head", split_axis=1, concat_axis=0, tiled=True)
-    whole_pairs = lax.all_gather(key_values, "head", axis=0, tiled=True)
+    whole_pairs = jnp.concatenate(
+        lax.all_to_all(jnp.stack([key_values] * lax.axis_size("head")), "head", 0, 0), axis=0
+    )
     my_kv = lax.dynamic_slice_in_dim(kv_index, group_rank * group_size, group_size)
     my_pairs = jnp.take(whole_pairs.reshape(tok_dev, 2, KVH, DH), my_kv, axis=2)
     earlier = []

time: 334 us -> 322 us (0.964)
  waiting for transfers between devices: 99.8 us -> 77.9 us
  starting transfers between devices: 16.3 us -> 25.1 us
    all_gather x1 -> x0, waiting for transfers between devices: 32.1 us -> none  [body(): whole_pairs = lax.all_gather(key_values, 'head', axis=0, tiled=True)]
    all_to_all x0 -> x1, waiting for transfers between devices: none -> 11.6 us  [body(): lax.all_to_all(jnp.stack([key_values] * lax.axis_size('head')), 'head', 0...]
    all_to_all x0 -> x1, starting transfers between devices: none -> 10.3 us  [body(): lax.all_to_all(jnp.stack([key_values] * lax.axis_size('head')), 'head', 0...]
where the time goes in v1:
time: 322 us; the launch traced here: 320 us
  waiting for transfers between devices  77.9 us (24%)
  local copies, waits for them, and re-layouts  56.7 us (18%)
  blocking collectives  48.1 us (15%)
  matrix products  47.1 us (15%)
  loops' own time  27.9 us (9%)
  starting transfers between devices  25.1 us (8%)
  other arithmetic  22.4 us (7%)
  between operations  14.3 us (4%)
    all_gather x1, waiting for transfers between devices, body(): lax.all_gather(packed[None], 'seq', axis=0, tiled=True)  59.9 us
    unnamed x1, blocking collectives  48.1 us
    dot_general x16, matrix products, block_attend(): jnp.einsum('qd,skd->qsk', q_rows, vert_keys, preferred_element_type=jnp.f...  30.9 us
    another operation x4, loops' own time, head_pass(): return lax.map(query_pass, (head_queries, block_range))  21 us
    dynamic_slice x20, local copies, waits for them, and re-layouts, body(): lax.map(head_pass, jnp.arange(group_size, dtype=jnp.int32))  12.1 us
    all_to_all x1, waiting for transfers between devices, body(): lax.all_to_all(jnp.stack([key_values] * lax.axis_size('head')), 'head', 0...  11.6 us
    reduce_sum x32, other arithmetic, block_attend(): row_total = jnp.sum(vert_exp, axis=(1, 2)) + jnp.sum(slash_exp, axis=(1, 2))  10.5 us
    all_to_all x1, starting transfers between devices, body(): lax.all_to_all(jnp.stack([key_values] * lax.axis_size('head')), 'head', 0...  10.3 us
  transfers between devices with their start and end apart: 6, of which 3 were waited for; matrix products, arithmetic and copies ran while one was open for 3% of the time, Pallas kernels for 0%

profile of v1, /device:TPU:1, one launch (start us, length us, event | category | flops | bytes accessed | tf_op | source)
XLA Modules:
  0.0 319.5 jit_solution(15277183083690456797)
XLA Ops:
  6.5 1.0 copy.61
  7.5 1.1 stack.2
  8.6 10.3 %all-to-all-start.1 = ((bf16[8,32,2,1024]{3,1,2,0:T(8,128)(2,1)}), bf16[8,32,2,1024]{3,1,2,0:T(8,128)(2,1)S(1)}, u32[]{:S(2)}, u32[]{:S(2)}) async-start(bf16[8,32,2,1024]{3,1,2,0:T(8,128)(2,1)} %stack.2), calls=%async_computation.1 | async-start | bytes 2097152 | tf_op jit(solution)/shard_map/all_to_all | solution.py:91
  19.0 1.6 sort.17
  22.4 11.6 %all-to-all-done.1 = bf16[8,32,2,1024]{3,1,2,0:T(8,128)(2,1)S(1)} async-done(((bf16[8,32,2,1024]{3,1,2,0:T(8,128)(2,1)}), bf16[8,32,2,1024]{3,1,2,0:T(8,128)(2,1)S(1)}, u32[]{:S(2)}, u32[]{:S(2)}) %all-to-all-start.1) | async-done | bytes 1048608 | tf_op jit(solution)/shard_map/all_to_all | solution.py:91
  38.0 4.3 %all-to-all-start = ((bf16[32,32,128]{2,0,1:T(8,128)(2,1)}), bf16[32,32,128]{2,0,1:T(8,128)(2,1)S(1)}, u32[]{:S(2)}, u32[]{:S(2)}) async-start(bf16[32,32,128]{2,0,1:T(8,128)(2,1)} %select_bitcast_fusion), calls=%async_computation | async-start | bytes 524288 | tf_op jit(solution)/shard_map/all_to_all | solution.py:89
  43.1 1.3 collective-permute-start
  44.4 4.0 %collective-permute-start.1 = (bf16[256,2,4,128]{3,0,1,2:T(8,128)(2,1)S(1)}, bf16[256,2,4,128]{3,0,1,2:T(8,128)(2,1)S(1)}, u32[]{:S(2)}, u32[]{:S(2)}) collective-permute-start(bf16[256,2,4,128]{3,0,1,2:T(8,128)(2,1)S(1)} %bitcast_select_fusion), channel_id=1, source_target_pairs={{0,8},{8,16},{16,24},{24,32},{32,40},{40,48},{48,56},{56,64},{64,7... | collective-permute-start | bytes 1572872 | tf_op jit(solution)/shard_map/ppermute | solution.py:17
  48.5 1.3 dynamic-slice
  50.7 48.1 %all-reduce = s32[256]{0:T(256)S(1)} all-reduce(s32[256]{0:T(256)S(1)} %dynamic-update-slice), channel_id=3, replica_groups=mesh['seq'=64,'head'=8] {'seq'}, use_global_device_ids=true, to_apply=%add | all-reduce | flops 256 | bytes 2048
  99.8 1.3 pad_maximum_fusion
  101.1 59.9 %all-gather.4.cloned.1.call-done = bf16[256,2,64,128]{3,2,1,0:T(8,128)(2,1)} async-done(((bf16[4,2,64,128]{3,2,1,0:T(8,128)(2,1)}), bf16[256,2,64,128]{3,2,1,0:T(8,128)(2,1)}) %all-gather.4.cloned.1.call-update) | async-done | bytes 8388624 | tf_op jit(solution)/shard_map/all_gather | solution.py:113
  161.0 136.6 %while.37 = (s32[]{:T(128)}, bf16[4,4,64,128]{3,2,1,0:T(8,128)(2,1)}, s32[4]{0:T(128)S(1)}, bf16[256,4,128]{2,0,1:T(8,128)(2,1)S(1)}, s32[4,8]{1,0:T(4,128)S(1)}...) while((s32[]{:T(128)}, ...), condition=%wide.region_11.12_spmd.clone.clone, body=%wide.region_3.11_spmd.clone.clone.sunk | while | flops 154098576 | bytes 21907556 | solution.py:157
  163.2 1.8 copy_bitcast_fusion.6
  165.0 1.5 slice_bitcast_fusion.8
  166.5 1.0 copy_bitcast_fusion.7
  168.8 25.7 %while.38 = (s32[]{:T(128)}, bf16[4,64,128]{2,1,0:T(8,128)(2,1)S(1)}, s32[64]{0:T(128)S(1)}, s32[4]{0:T(128)S(1)}, s32[]{:T(128)}, /*index=5*/s32[8]{0:T(128)S(1...) while((s32[]{:T(128)}, ...), condition=%wide.region_10.10_spmd, body=%wide.region_4.9_spmd.sunk | while | flops 154098560 | bytes 12468941 | solution.py:155
  170.2 1.9 fusion.56
  176.6 1.9 fusion.56
  183.0 1.9 fusion.56
  189.4 1.9 fusion.56
  197.3 1.8 copy_bitcast_fusion.6
  199.1 1.5 slice_bitcast_fusion.8
  200.6 1.0 copy_bitcast_fusion.7
  202.9 25.7 %while.38 = (s32[]{:T(128)}, bf16[4,64,128]{2,1,0:T(8,128)(2,1)S(1)}, s32[64]{0:T(128)S(1)}, s32[4]{0:T(128)S(1)}, s32[]{:T(128)}, /*index=5*/s32[8]{0:T(128)S(1...) while((s32[]{:T(128)}, ...), condition=%wide.region_10.10_spmd, body=%wide.region_4.9_spmd.sunk | while | flops 154098560 | bytes 12468941 | solution.py:155
  204.3 1.9 fusion.56
  210.7 1.9 fusion.56
  217.2 1.9 fusion.56
  223.6 1.9 fusion.56
  231.5 1.8 copy_bitcast_fusion.6
  233.3 1.5 slice_bitcast_fusion.8
  234.7 1.0 copy_bitcast_fusion.7
  237.1 25.7 %while.38 = (s32[]{:T(128)}, bf16[4,64,128]{2,1,0:T(8,128)(2,1)S(1)}, s32[64]{0:T(128)S(1)}, s32[4]{0:T(128)S(1)}, s32[]{:T(128)}, /*index=5*/s32[8]{0:T(128)S(1...) while((s32[]{:T(128)}, ...), condition=%wide.region_10.10_spmd, body=%wide.region_4.9_spmd.sunk | while | flops 154098560 | bytes 12468941 | solution.py:155
  238.4 1.9 fusion.56
  244.9 1.9 fusion.56
  251.3 1.9 fusion.56
  257.7 1.9 fusion.56
  265.6 1.8 copy_bitcast_fusion.6
  267.4 1.5 slice_bitcast_fusion.8
  268.9 1.0 copy_bitcast_fusion.7
  271.2 25.7 %while.38 = (s32[]{:T(128)}, bf16[4,64,128]{2,1,0:T(8,128)(2,1)S(1)}, s32[64]{0:T(128)S(1)}, s32[4]{0:T(128)S(1)}, s32[]{:T(128)}, /*index=5*/s32[8]{0:T(128)S(1...) while((s32[]{:T(128)}, ...), condition=%wide.region_10.10_spmd, body=%wide.region_4.9_spmd.sunk | while | flops 154098560 | bytes 12468941 | solution.py:155
  272.6 1.9 fusion.56
  279.0 1.9 fusion.56
  285.4 1.9 fusion.56
  291.9 1.9 fusion.56
  297.6 1.9 copy.68
  299.5 5.2 %all-to-all-start.2 = ((bf16[4,256,128]{2,0,1:T(4,128)(2,1)}), bf16[4,256,128]{2,0,1:T(4,128)(2,1)S(1)}, u32[]{:S(2)}, u32[]{:S(2)}) async-start(bf16[4,256,128]{2,0,1:T(4,128)(2,1)} %bitcast.25), calls=%async_computation.2 | async-start | bytes 524288 | tf_op jit(solution)/shard_map/all_to_all | solution.py:160
  304.7 6.4 %all-to-all-done.2 = bf16[4,256,128]{2,0,1:T(4,128)(2,1)S(1)} async-done(((bf16[4,256,128]{2,0,1:T(4,128)(2,1)}), bf16[4,256,128]{2,0,1:T(4,128)(2,1)S(1)}, u32[]{:S(2)}, u32[]{:S(2)}) %all-to-all-start.2) | async-done | bytes 262176 | tf_op jit(solution)/shard_map/all_to_all | solution.py:160
  (400 shorter events, 70.0 us)
Async XLA Ops:
  6.5 30.0 %copy-start = (bf16[32,4096]{1,0:T(8,128)(2,1)S(1)}, bf16[32,4096]{1,0:T(8,128)(2,1)}, u32[]{:S(2)}) copy-start(bf16[32,4096]{1,0:T(8,128)(2,1)} %param.10) | copy-start | bytes 786436
  6.5 12.4 %copy-start.1 = (s32[32]{0:T(128)S(1)}, s32[32]{0:T(128)}, u32[]{:S(2)}) copy-start(s32[32]{0:T(128)} %param.15) | copy-start | bytes 388
  6.5 14.9 %copy-start.4 = (s32[32,16]{0,1:T(8,128)S(1)}, s32[32,16]{0,1:T(8,128)}, u32[]{:S(2)}) copy-start(s32[32,16]{0,1:T(8,128)} %param.13) | copy-start | bytes 6148
  8.6 25.3 %all-to-all-start.1 = ((bf16[8,32,2,1024]{3,1,2,0:T(8,128)(2,1)}), bf16[8,32,2,1024]{3,1,2,0:T(8,128)(2,1)S(1)}, u32[]{:S(2)}, u32[]{:S(2)}) async-start(bf16[8,32,2,1024]{3,1,2,0:T(8,128)(2,1)} %stack.2), calls=%async_computation.1 | async-start | bytes 2097152 | tf_op jit(solution)/shard_map/all_to_all | solution.py:91
  18.9 142.1 %all-gather.4.cloned.1.call-start = ((), (), s32[]{:S(2)}) async-start(), calls=%async_computation.3 | async-start | bytes 8519680 | tf_op jit(solution)/shard_map/all_gather | solution.py:113
  35.8 63.2 %copy-start.5 = (s32[32,8]{0,1:T(8,128)S(1)}, s32[32,8]{0,1:T(8,128)}, u32[]{:S(2)}) copy-start(s32[32,8]{0,1:T(8,128)} %param.14) | copy-start | bytes 3076
  38.0 61.7 %all-to-all-start = ((bf16[32,32,128]{2,0,1:T(8,128)(2,1)}), bf16[32,32,128]{2,0,1:T(8,128)(2,1)S(1)}, u32[]{:S(2)}, u32[]{:S(2)}) async-start(bf16[32,32,128]{2,0,1:T(8,128)(2,1)} %select_bitcast_fusion), calls=%async_computation | async-start | bytes 524288 | tf_op jit(solution)/shard_map/all_to_all | solution.py:89
  43.1 56.7 %collective-permute-start = (bf16[256,2,4,128]{3,0,1,2:T(8,128)(2,1)S(1)}, bf16[256,2,4,128]{3,0,1,2:T(8,128)(2,1)S(1)}, u32[]{:S(2)}, u32[]{:S(2)}) collective-permute-start(bf16[256,2,4,128]{3,0,1,2:T(8,128)(2,1)S(1)} %bitcast_select_fusion), channel_id=1, source_target_pairs={{0,16},{8,24},{16,32},{24,40},{32,48},{40,56},{48,64},{56,72},{64,... | collective-permute-start | bytes 1572872 | tf_op jit(solution)/shard_map/ppermute | solution.py:17
  44.4 55.4 %collective-permute-start.1 = (bf16[256,2,4,128]{3,0,1,2:T(8,128)(2,1)S(1)}, bf16[256,2,4,128]{3,0,1,2:T(8,128)(2,1)S(1)}, u32[]{:S(2)}, u32[]{:S(2)}) collective-permute-start(bf16[256,2,4,128]{3,0,1,2:T(8,128)(2,1)S(1)} %bitcast_select_fusion), channel_id=1, source_target_pairs={{0,8},{8,16},{16,24},{24,32},{32,40},{40,48},{48,56},{56,64},{64,7... | collective-permute-start | bytes 1572872 | tf_op jit(solution)/shard_map/ppermute | solution.py:17
  173.5 1.2 copy-start.2
  179.9 1.2 copy-start.2
  186.3 1.2 copy-start.2
  192.7 1.2 copy-start.2
  207.6 1.2 copy-start.2
  214.0 1.2 copy-start.2
  220.5 1.2 copy-start.2
  226.9 1.2 copy-start.2
  241.7 1.2 copy-start.2
  248.2 1.2 copy-start.2
  254.6 1.2 copy-start.2
  261.0 1.2 copy-start.2
  275.9 1.2 copy-start.2
  282.3 1.2 copy-start.2
  288.7 1.2 copy-start.2
  295.2 1.2 copy-start.2
  297.6 14.2 %copy-start.3 = (bf16[32,4096]{1,0:T(8,128)(2,1)S(1)}, bf16[32,4096]{1,0:T(8,128)(2,1)}, u32[]{:S(2)}) copy-start(bf16[32,4096]{1,0:T(8,128)(2,1)} %param.12) | copy-start | bytes 786436
  299.5 11.7 %all-to-all-start.2 = ((bf16[4,256,128]{2,0,1:T(4,128)(2,1)}), bf16[4,256,128]{2,0,1:T(4,128)(2,1)S(1)}, u32[]{:S(2)}, u32[]{:S(2)}) async-start(bf16[4,256,128]{2,0,1:T(4,128)(2,1)} %bitcast.25), calls=%async_computation.2 | async-start | bytes 524288 | tf_op jit(solution)/shard_map/all_to_all | solution.py:160
Sparse Core Ops, SparseCore 0:
  36.6 124.3 all-gather.3
